TPU v7x, 256 devices: a whole 4x4x8 slice. The times are simulated.
256 devices in a mesh: sweep: 16 (over z, y_hi), cross: 16 (over y_lo, x, core).
Axes of the slice: x: 4, y: 4 (y_hi: 2, y_lo: 2; y = y_hi * 2 + y_lo), z: 8, core: 2. Of those that a mesh axis runs over, the one named last changes fastest.
Arguments:
- right_side: bfloat16 [32, 64, 320, 128], P('sweep', 'cross'), may hold values from -6 to 6
- diag_inv: bfloat16 [32, 64, 320, 320], P('sweep', 'cross')
- diag_blk: bfloat16 [32, 64, 320, 320], P('sweep', 'cross')
- lower_blk: bfloat16 [32, 64, 320, 320], P('sweep', 'cross')
- upper_blk: bfloat16 [32, 64, 320, 320], P('sweep', 'cross')
- cross_minus: bfloat16 [32, 64, 320, 320], P('sweep', 'cross')
- cross_plus: bfloat16 [32, 64, 320, 320], P('sweep', 'cross')
- elem_slot: int32 [32, 64], P('sweep', 'cross'), may hold values from 0 to 7, as said below
Outputs:
- precond: bfloat16 [32, 64, 320, 128], P('sweep', 'cross')
- jacobian_prod: bfloat16 [32, 64, 320, 128], P('sweep', 'cross')
Inputs may be any that keep to these rules, and one draw needn't show every extreme that they name: `elem_slot`: within each aligned block of 2 slabs by 4 pencils the entries are a permutation of 0 to 7.
All inputs are finite; a program needn't handle non-finite values.
Results may differ from a plain program's by a relative error of at most 0.0083.
Values may be sent and summed in bfloat16 or wider, within the bound.
No kernel may reach another device: no remote copies, remote signals or barrier semaphores. Data moves between devices by JAX's collectives and lax.ppermute only.
A program may use at most 256 MiB of HBM per device.

v0:
```python
import functools

import jax
import jax.numpy as jnp
from jax import lax
from jax.experimental import pallas as pl
from jax.experimental.pallas import tpu as pltpu
from jax.sharding import PartitionSpec as P

BF = jnp.bfloat16
F32 = jnp.float32
GROUP = 4
VMEM_LIMIT = 28 << 20
LONG = pl.CostEstimate(flops=10**10, transcendentals=0, bytes_accessed=1024)
SHORT = pl.CostEstimate(flops=1024, transcendentals=0, bytes_accessed=1024)


def mm(a, b):
    return jnp.dot(a, b, preferred_element_type=F32)


def mm_fine(a, x):
    width = x.shape[1]
    top = x.astype(BF)
    rest = (x - top.astype(F32)).astype(BF)
    both = mm(a, jnp.concatenate([top, rest], axis=1))
    return both[:, :width] + both[:, width:]


def packed_rows(n):
    return 2 * n + n // 2


def pack(ref, base, mat):
    n = mat.shape[0]
    half = n // 2
    ref[base : base + n, :] = mat[:, 0:128]
    ref[base + n : base + 2 * n, :] = mat[:, 128:256]
    ref[base + 2 * n : base + 2 * n + half, 0:64] = mat[0:half, 256:320]
    ref[base + 2 * n : base + 2 * n + half, 64:128] = mat[half:n, 256:320]


def unpack(ref, base, n):
    half = n // 2
    tail = ref[base + 2 * n : base + 2 * n + half, :]
    last = jnp.concatenate([tail[:, 0:64], tail[:, 64:128]], axis=0)
    return jnp.concatenate(
        [ref[base : base + n, :], ref[base + n : base + 2 * n, :], last], axis=1
    )


def map_rows(n):
    return 3 * packed_rows(n) + 2 * n


def local_map_kernel(slots, place, d0, d1, l0, l1, u0, u1, r0, r1, out):
    n = d0.shape[0]
    rows = packed_rows(n)
    inv0, inv1 = d0[...], d1[...]
    e0 = mm(inv0, l0[...])
    e1 = mm(inv1, l1[...]).astype(BF)
    h0 = mm(inv0, u0[...]).astype(BF)
    h1 = mm(inv1, u1[...]).astype(BF)
    y0 = mm(inv0, r0[...])
    y1 = mm(inv1, r1[...])
    a = mm(e1, e0.astype(BF)).astype(BF)
    c = y1 - mm_fine(e1, y0)
    b = mm(h0, h1).astype(BF)
    g = -(e0 + mm(h0, a))
    h = y0 - mm_fine(h0, c)
    pack(out, 0, a)
    pack(out, rows, b)
    pack(out, 2 * rows, g.astype(BF))
    out[3 * rows : 3 * rows + n, :] = c.astype(BF)
    out[3 * rows + n : 3 * rows + 2 * n, :] = h.astype(BF)


def stored(slab, pencil, height, width):
    return pl.BlockSpec(
        (None, height, width), lambda i, sl, at: (sl[slab, pencil(at)], 0, 0)
    )


def constant(shape):
    return pl.BlockSpec(shape, lambda i, sl, at: (0,) * len(shape))


def element_call(kernel, in_specs, out_shape, slots, place, *operands, name, cost=SHORT):
    return pl.pallas_call(
        kernel,
        grid_spec=pltpu.PrefetchScalarGridSpec(
            num_scalar_prefetch=2,
            grid=(1,),
            in_specs=in_specs,
            out_specs=[constant(o.shape) for o in out_shape],
        ),
        out_shape=out_shape,
        compiler_params=pltpu.CompilerParams(vmem_limit_bytes=VMEM_LIMIT),
        cost_estimate=cost,
        name=name,
    )(slots, place, *operands)


def local_map(slots, place, diag_inv, lower, upper, source, distance):
    n, cols = source.shape[1:]

    def pencil(at):
        return lax.bitwise_xor(at[3], jnp.int32(distance))

    (out,) = element_call(
        local_map_kernel,
        [stored(s, pencil, n, n) for s in (0, 1, 0, 1, 0, 1)]
        + [stored(s, pencil, n, cols) for s in (0, 1)],
        [jax.ShapeDtypeStruct((map_rows(n), cols), BF)],
        slots, place, diag_inv, diag_inv, lower, lower, upper, upper, source, source,
        name="local_map",
    )
    return out


def halves(x):
    top = x.astype(BF)
    return top, (x - top.astype(F32)).astype(BF)


def prepare_kernel(slots, place, *refs):
    d0, d1, l0, l1, u0, u1, r0, r1 = refs[0:8]
    diags, minuses, pluses = refs[8:10], refs[10:12], refs[12:14]
    out, first_ops, second_ops, c_out, y_out, rows_out, lowers, sides = refs[14:]
    n = d0.shape[0]
    pencil = pl.program_id(0)
    for s in range(2):
        row = (diags[s], (l0, l1)[s], (u0, u1)[s], minuses[s], pluses[s])
        for t, block in enumerate(row):
            rows_out[s, :, t * n : (t + 1) * n] = block[...]
    lowers[...] = l0[...]

    @pl.when(pencil == 0)
    def _():
        for s in range(2):
            sides[s] = minuses[s][...]

    @pl.when(pencil == GROUP - 1)
    def _():
        for s in range(2):
            sides[s + 2] = pluses[s][...]

    rows = packed_rows(n)
    inv0, inv1 = d0[...], d1[...]
    e0 = mm(inv0, l0[...])
    e0_top, e0_rest = halves(e0)
    e1_top, e1_rest = halves(mm(inv1, l1[...]))
    h0_top, h0_rest = halves(mm(inv0, u0[...]))
    h1_top, h1_rest = halves(mm(inv1, u1[...]))
    y0 = mm(inv0, r0[...])
    a = mm(e1_top, e0_top) + (mm(e1_top, e0_rest) + mm(e1_rest, e0_top))
    c = mm(inv1, r1[...]) - (mm_fine(e1_top, y0) + mm(e1_rest, y0.astype(BF)))
    a_top, a_rest = halves(a)
    for t, part in enumerate((a_top, a_rest, -h1_top, -h1_rest)):
        first_ops[:, t * n : (t + 1) * n] = part
    for t, part in enumerate((-e0_top, -e0_rest, -h0_top, -h0_rest, -h0_top)):
        second_ops[:, t * n : (t + 1) * n] = part
    c_out[...] = c
    y_out[...] = y0

    @pl.when(pencil == place[3])
    def _():
        pack(out, 0, a_top)
        pack(out, rows, mm(h0_top, h1_top).astype(BF))
        pack(out, 2 * rows, (-(e0 + mm(h0_top, a_top))).astype(BF))
        out[3 * rows : 3 * rows + n, :] = c.astype(BF)
        out[3 * rows + n : 3 * rows + 2 * n, :] = (y0 - mm_fine(h0_top, c)).astype(BF)


def prepare(slots, place, diag_inv, lower, upper, source, diagonal, minus, plus):
    n, cols = source.shape[1:]

    def block(slab, width):
        return pl.BlockSpec((None, n, width), lambda p, sl, at: (sl[slab, p], 0, 0))

    def per(width):
        return pl.BlockSpec((None, n, width), lambda p, sl, at: (p, 0, 0))

    shape = jax.ShapeDtypeStruct
    return pl.pallas_call(
        prepare_kernel,
        grid_spec=pltpu.PrefetchScalarGridSpec(
            num_scalar_prefetch=2,
            grid=(GROUP,),
            in_specs=[block(s, n) for s in (0, 1) * 3]
            + [block(s, cols) for s in (0, 1)]
            + [block(s, n) for s in (0, 1) * 3],
            out_specs=[
                pl.BlockSpec((map_rows(n), cols), lambda p, sl, at: (0, 0)),
                per(4 * n), per(5 * n), per(cols), per(cols),
                pl.BlockSpec((None, 2, n, 5 * n), lambda p, sl, at: (p, 0, 0, 0)),
                per(n),
                pl.BlockSpec((4, n, n), lambda p, sl, at: (0, 0, 0)),
            ],
        ),
        out_shape=[
            shape((map_rows(n), cols), BF),
            shape((GROUP, n, 4 * n), BF),
            shape((GROUP, n, 5 * n), BF),
            shape((GROUP, n, cols), F32),
            shape((GROUP, n, cols), F32),
            shape((GROUP, 2, n, 5 * n), BF),
            shape((GROUP, n, n), BF),
            shape((4, n, n), BF),
        ],
        compiler_params=pltpu.CompilerParams(vmem_limit_bytes=VMEM_LIMIT),
        cost_estimate=SHORT,
        name="prepare",
    )(
        slots, place, diag_inv, diag_inv, lower, lower, upper, upper, source, source,
        diagonal, diagonal, minus, minus, plus, plus,
    )


def per_owner(place, pieces, body):
    for owned in range(GROUP):

        @pl.when(place[3] == owned)
        def _(owned=owned):
            body([pieces[owned ^ j] for j in range(GROUP)], owned)


def segment(one, n):
    rows = packed_rows(n)
    return (
        unpack(one, 0, n),
        unpack(one, rows, n),
        unpack(one, 2 * rows, n),
        one[3 * rows : 3 * rows + n, :].astype(F32),
        one[3 * rows + n : 3 * rows + 2 * n, :].astype(F32),
    )


def group_back_kernel(
    place, across, near, next_one, own, a_low, b_out, c_low, g_out, h_out, send_far
):
    n = a_low.shape[0]

    def body(maps, owned):
        (a0, b0, g0, c0, h0), (a1, b1, g1, c1, h1), (a2, b2, g2, c2, h2), (_, b3, g3, _, h3) = (
            segment(one, n) for one in maps
        )
        a = mm(a1, a0).astype(BF)
        b = mm(b0, b1).astype(BF)
        c = mm_fine(a1, c0) + c1
        low_g = mm(b0, mm(g1, a0).astype(BF)) + g0.astype(F32)
        high_g = (mm(b2, mm(g3, a2).astype(BF)) + g2.astype(F32)).astype(BF)
        g = (mm(b, mm(high_g, a).astype(BF)) + low_g).astype(BF)
        low_h = mm_fine(b0, mm_fine(g1, c0) + h1) + h0
        high_h = mm_fine(b2, mm_fine(g3, c2) + h3) + h2
        h = mm_fine(b, mm_fine(high_g, c) + high_h) + low_h
        a_low[...] = a
        c_low[...] = c
        g_out[...] = g
        h_out[...] = h
        send_far[0:n, :] = h.astype(BF)
        through = mm(b, mm(b2, b3).astype(BF)).astype(BF)
        b_out[...] = through
        pack(send_far, n, jnp.where(place[4] == 1, through, g))

    per_owner(place, (own, near, next_one, across), body)


def group_front_kernel(
    place, across, near, next_one, own, a_low, c_low, send, a_out, c_out
):
    n = a_low.shape[0]

    def body(maps, owned):
        (a2, _, _, c2, _), (a3, _, _, c3, _) = (segment(one, n) for one in maps[2:])
        a = mm(a3, a2).astype(BF)
        c = mm_fine(a, c_low[...]) + (mm_fine(a3, c2) + c3)
        send[...] = c.astype(BF)
        c_out[...] = c
        a_out[...] = mm(a, a_low[...]).astype(BF)

    per_owner(place, (own, near, next_one, across), body)


def forward_one_kernel(incoming, a, c, g, h, send, inner):
    send[...] = (mm(a[...], incoming[...]) + c[...]).astype(BF)
    inner[...] = (mm(g[...], incoming[...]) + h[...]).astype(BF)


def turn_kernel(incoming, far, a, b, g, c, h, send, back_in):
    n = a.shape[0]
    front = incoming[...]
    ahead = mm(a[...], front) + c[...]
    back = mm_fine(unpack(far, n, n), ahead) + far[0:n, :].astype(F32)
    send[...] = (mm_fine(b[...], back) + (mm(g[...], front) + h[...])).astype(BF)
    back_in[...] = back.astype(BF)


def through_group(maps, first, n):
    rows = packed_rows(n)
    fronts, inner = [first], [None]
    for one in maps[:-1]:
        shift = one[3 * rows : 3 * rows + n, :].astype(F32)
        fronts.append(mm_fine(unpack(one, 0, n), fronts[-1]) + shift)
    for one, front in zip(maps[1:], fronts[1:]):
        shift = one[3 * rows + n : 3 * rows + 2 * n, :].astype(F32)
        inner.append(mm_fine(unpack(one, 2 * rows, n), front) + shift)
    return fronts, inner


def entering_kernel(
    place, across, near, next_one, own, hop1, hop2, fronts_out, inner_out, leaving, maps
):
    n = hop1.shape[0]
    rows = packed_rows(n)
    which = place[4]
    for distance, piece in enumerate((own, near, next_one, across)):
        maps[lax.bitwise_xor(place[3], jnp.int32(distance))] = piece[...]
    zero = jnp.zeros_like(hop1[...])
    first = jnp.where(which == 1, hop1[...], jnp.where(which == 2, hop2[...], zero)).astype(F32)
    ordered = [maps.at[j] for j in range(GROUP)]
    fronts, inner = through_group(ordered, first, n)
    for j in range(GROUP):
        fronts_out[j] = fronts[j].astype(BF)
        if j:
            inner_out[j] = inner[j]
    shift = ordered[-1][3 * rows : 3 * rows + n, :].astype(F32)
    leaving[...] = (mm_fine(unpack(ordered[-1], 0, n), fronts[-1]) + shift).astype(BF)


def interfaces_kernel(
    place, maps, far, inner_one, hop_three, hop_one, back_two, hop_zero,
    fronts_in, inner_in, out_near, out_next, out_across, out_own, fronts_now, inner_now, backs,
):
    n = hop_one.shape[0]
    rows = packed_rows(n)
    which = place[4]
    zero = jnp.zeros_like(hop_one[...])
    through_one = mm(unpack(far, n, n), hop_zero[...]) + inner_one[...].astype(F32)
    back = jnp.where(
        which == 0, through_one.astype(BF),
        jnp.where(which == 1, hop_one[...], jnp.where(which == 2, back_two[...], zero)),
    ).astype(F32)
    ordered = [maps.at[j] for j in range(GROUP)]

    @pl.when(which == GROUP - 1)
    def _():
        fronts, inner = through_group(ordered, hop_three[...].astype(F32), n)
        for j in range(GROUP):
            fronts_now[j] = fronts[j].astype(BF)
            if j:
                inner_now[j] = inner[j]

    @pl.when(which != GROUP - 1)
    def _():
        for j in range(GROUP):
            fronts_now[j] = fronts_in[j]
            if j:
                inner_now[j] = inner_in[j]

    for j in reversed(range(GROUP)):
        backs[j] = back.astype(BF)
        if j:
            back = mm_fine(unpack(ordered[j], rows, n), back) + inner_now[j]
    for distance, out in enumerate((out_own, out_near, out_next, out_across)):
        peer = lax.bitwise_xor(place[3], jnp.int32(distance))
        out[0:n, :] = fronts_now[peer]
        out[n : 2 * n, :] = backs[peer]


def whole_call(kernel, outs, scalars, *operands, name, cost=SHORT, scratch=()):
    specs = [pl.BlockSpec(memory_space=pltpu.SMEM)] * len(scalars)
    specs += [pl.BlockSpec(memory_space=pltpu.VMEM)] * len(operands)
    return pl.pallas_call(
        kernel,
        in_specs=specs,
        out_specs=[pl.BlockSpec(memory_space=pltpu.VMEM)] * len(outs),
        out_shape=[jax.ShapeDtypeStruct(s, d) for s, d in outs],
        scratch_shapes=scratch,
        compiler_params=pltpu.CompilerParams(vmem_limit_bytes=VMEM_LIMIT),
        cost_estimate=cost,
        name=name,
    )(*scalars, *operands)


def finish_second_kernel(
    place, near, next_one, across, own, first_ops, c, tops, rests, fronts, backs
):
    n = c.shape[1]
    for distance, piece in enumerate((own, near, next_one, across)):
        pencil = lax.bitwise_xor(place[3], jnp.int32(distance))
        fronts[pencil] = piece[0:n, :]
        backs[pencil] = piece[n : 2 * n, :]
    for p in range(GROUP):
        front = fronts[p]
        back = backs[p]
        x1 = c[p] + mm(first_ops[p], jnp.concatenate([front, front, back, back], axis=0))
        tops[p], rests[p] = halves(x1)


def finish_first_kernel(place, fronts, second_ops, y0, tops, rests, beside, firsts):
    n = y0.shape[1]
    for p in range(GROUP):
        front = fronts[p]
        top = tops[p]
        around = jnp.concatenate([front, front, top, top, rests[p]], axis=0)
        firsts[p] = (y0[p] + mm(second_ops[p], around)).astype(BF)
    even = lax.rem(place[1], 2) == 0
    for s, values in enumerate((firsts, tops)):
        beside[s] = jnp.where(even, values[0], values[GROUP - 1])


def row_products(chosen, rows, firsts, tops, backs, partial):
    n = tops.shape[1]
    zero = jnp.zeros(tops.shape[1:], BF)

    def value(s, p):
        if p < 0 or p >= GROUP or s < 0:
            return zero
        return backs[p] if s == 2 else (firsts, tops)[s][p]

    for i, p in enumerate(chosen):
        for s in range(2):
            around = [value(s, p), value(s - 1, p), value(s + 1, p), value(s, p - 1), value(s, p + 1)]
            partial[i, s] = mm(rows[p, s], jnp.concatenate(around, axis=0))


def first_rows_kernel(place, rows, firsts, tops, backs, within, partial):
    even = lax.rem(place[1], 2) == 0
    row_products((0, 1), rows, firsts, tops, backs, partial)
    for s, values in enumerate((firsts, tops)):
        within[s] = jnp.where(even, values[GROUP - 1], values[0])


def second_rows_kernel(slots, rows, firsts, tops, backs, precond, partial):
    row_products((2, 3), rows, firsts, tops, backs, partial)
    for s in range(2):
        for p in range(GROUP):
            precond[slots[s, p]] = (firsts, tops)[s][p]


def edge_jacobian_kernel(slots, place, beside, below, within, partial_a, partial_b, lowers, sides, jac):
    even = lax.rem(place[1], 2) == 0
    low = [jnp.where(even, beside[s], within[s]) for s in range(2)]
    high = [jnp.where(even, within[s], beside[s]) for s in range(2)]
    left = jnp.where(place[1] == 0, 0.0, 1.0).astype(F32)
    right = jnp.where(place[1] == place[2] - 1, 0.0, 1.0).astype(F32)
    start = jnp.where(place[0] == 0, 0.0, 1.0).astype(F32)
    for s in range(2):
        for p in range(GROUP):
            total = partial_a[p, s] if p < 2 else partial_b[p - 2, s]
            if s == 0:
                total = total + start * mm(lowers[p], below[p])
            if p == 0:
                total = total + left * mm(sides[s], low[s])
            if p == GROUP - 1:
                total = total + right * mm(sides[s + 2], high[s])
            jac[slots[s, p]] = total.astype(BF)


def local(right_side, diag_inv, diag_blk, lower_blk, upper_blk, cross_minus, cross_plus, elem_slot):
    n, cols = right_side.shape[2:]
    source, inverse, diagonal, lower, upper, minus, plus = (
        pltpu.with_memory_space_constraint(
            values.reshape((-1,) + values.shape[2:]), pltpu.HBM
        )
        for values in (
            right_side, diag_inv, diag_blk, lower_blk, upper_blk, cross_minus, cross_plus
        )
    )
    count = lax.axis_size("sweep")
    across = lax.axis_size("cross")
    sweep_at = lax.axis_index("sweep")
    place = jnp.stack(
        [
            sweep_at, lax.axis_index("cross"), jnp.int32(across),
            lax.rem(sweep_at, GROUP), lax.div(sweep_at, GROUP),
        ]
    ).astype(jnp.int32)
    def hop(values, *moves):
        pairs = [(a * GROUP + k, b * GROUP + k) for a, b in moves for k in range(GROUP)]
        return lax.ppermute(values, "sweep", pairs)

    def to_peer(values, distance):
        return lax.ppermute(values, "sweep", [(i, i ^ distance) for i in range(count)])

    vec, vec32, mat = ((n, cols), BF), ((n, cols), F32), ((n, n), BF)
    maps = [None] * GROUP
    for distance in (3, 1, 2):
        piece = local_map(elem_slot, place, inverse, lower, upper, source, distance)
        maps[distance] = to_peer(piece, distance)
    maps[0], first_ops, second_ops, c_own, y_own, rows, lowers, sides = prepare(
        elem_slot, place, inverse, lower, upper, source, diagonal, minus, plus
    )
    pieces = (maps[3], maps[1], maps[2], maps[0])

    a_low, b, c_low, g, h, send_far = whole_call(
        group_back_kernel, [mat, mat, vec32, mat, vec32, ((n + packed_rows(n), cols), BF)],
        [place], *pieces, name="group_back",
    )
    far = hop(send_far, (3, 2), (1, 0))
    send, a, c = whole_call(
        group_front_kernel, [vec, mat, vec32], [place],
        *pieces, a_low, c_low, name="group_front",
    )
    hop1 = hop(send, (0, 1))
    send, inner_one = whole_call(
        forward_one_kernel, [vec, vec], [], hop1, a, c, g, h, name="forward_one"
    )
    hop2 = hop(send, (1, 2))
    inner_one = hop(inner_one, (1, 0))
    send, back_two = whole_call(
        turn_kernel, [vec, vec], [], hop2, far, a, b, g, c, h, name="turn"
    )
    hop_zero = hop(send, (2, 0))
    hop_one = hop(send, (2, 1))
    fronts, inner, ahead, ordered = whole_call(
        entering_kernel,
        [
            ((GROUP, n, cols), BF), ((GROUP, n, cols), F32), vec,
            ((GROUP, map_rows(n), cols), BF),
        ],
        [place],
        *pieces, hop1, hop2, name="entering",
    )
    hop_three = hop(ahead, (2, 3))
    both = ((2 * n, cols), BF)
    ends = whole_call(
        interfaces_kernel, [both] * GROUP, [place], ordered, far, inner_one,
        hop_three, hop_one, back_two, hop_zero, fronts, inner, name="interfaces",
        scratch=[
            pltpu.VMEM((GROUP, n, cols), BF), pltpu.VMEM((GROUP, n, cols), F32),
            pltpu.VMEM((GROUP, n, cols), BF),
        ],
    )
    ends = [to_peer(values, distance) for distance, values in zip((1, 2, 3), ends)] + [ends[3]]

    pair = ((2, n, cols), BF)
    four = ((GROUP, n, cols), BF)
    tops, rests, fronts, backs = whole_call(
        finish_second_kernel, [four] * 4, [place], *ends, first_ops, c_own, name="finish_second"
    )
    below = lax.ppermute(tops, "sweep", [(i, (i + 1) % count) for i in range(count)])
    beside, firsts = whole_call(
        finish_first_kernel, [pair, four], [place],
        fronts, second_ops, y_own, tops, rests, name="finish_first",
    )
    aside = []
    for i in range(1, across - 1, 2):
        aside += [(i, i + 1), (i + 1, i)]
    beside = lax.ppermute(beside, "cross", aside)
    part = ((2, 2, n, cols), F32)
    within, partial_a = whole_call(
        first_rows_kernel, [pair, part], [place], rows, firsts, tops, backs, name="first_rows"
    )
    within = lax.ppermute(within, "cross", [(i, i ^ 1) for i in range(across)])
    every = ((2 * GROUP, n, cols), BF)
    precond, partial_b = whole_call(
        second_rows_kernel, [every, part], [elem_slot], rows, firsts, tops, backs, name="second_rows"
    )
    (jac,) = whole_call(
        edge_jacobian_kernel, [every], [elem_slot, place],
        beside, below, within, partial_a, partial_b, lowers, sides, name="edge_jacobian",
    )
    return precond.reshape(right_side.shape), jac.reshape(right_side.shape)


def solution(mesh):
    blocks = P("sweep", "cross", None, None)
    in_specs = (blocks,) * 7 + (P("sweep", "cross"),)
    return jax.shard_map(
        local, mesh=mesh, in_specs=in_specs, out_specs=(blocks, blocks), check_vma=False
    )
```

profile of v0, /device:TPU:8, one launch (start us, length us, event | category | flops | bytes accessed | tf_op | source)
XLA Modules:
  0.0 107.4 jit_solution(15284521549550524477)
XLA Ops:
  1.4 3.6 %local_map.3 = bf16[3040,128]{1,0:T(8,128)(2,1)S(1)} custom-call(s32[2,4]{1,0:T(2,128)S(1)} %copy-done, s32[5]{0:T(128)S(1)} %stack.19.place, bf16[8,320,320]{2,1,0:T(8,128)(2,1)} %bitcast.13, bf16[8,320,320]{2,1,0:T(8,128)(2,1)} %bitcast.14, bf16[8,320,320]{2,1,0:T(8,128)(2,1)} %bitcast.21, bf16[8,320,320]{2,1,0:T(8,128)(2,1)} %bitcast.22, ...), custom_call_target="tpu_custom_call" | custom-call | flops 1024 | bytes 1024 | tf_op jit(solution)/shard_map/local_map/pallas_call | solution.py:89
  5.0 3.7 %collective-permute-start = (bf16[3040,128]{1,0:T(8,128)(2,1)S(1)}, bf16[3040,128]{1,0:T(8,128)(2,1)S(1)}, u32[]{:S(2)}, u32[]{:S(2)}) collective-permute-start(bf16[3040,128]{1,0:T(8,128)(2,1)S(1)} %local_map.3), channel_id=1, source_target_pairs={{0,48},{16,32},{32,16},{48,0},{64,112},{80,96},{96,80},{112,64},{1... | collective-permute-start | bytes 2334728 | tf_op jit(solution)/shard_map/ppermute | solution.py:485
  8.8 3.6 %local_map.4 = bf16[3040,128]{1,0:T(8,128)(2,1)S(1)} custom-call(s32[2,4]{1,0:T(2,128)S(1)} %copy-done.1, s32[5]{0:T(128)S(1)} %stack.19.place, bf16[8,320,320]{2,1,0:T(8,128)(2,1)} %bitcast.15, bf16[8,320,320]{2,1,0:T(8,128)(2,1)} %bitcast.16, bf16[8,320,320]{2,1,0:T(8,128)(2,1)} %bitcast.23, bf16[8,320,320]{2,1,0:T(8,128)(2,1)} %bitcast.24, ...), custom_call_target="tpu_custom_call" | custom-call | flops 1024 | bytes 1024 | tf_op jit(solution)/shard_map/local_map/pallas_call | solution.py:89
  13.7 3.6 %local_map.5 = bf16[3040,128]{1,0:T(8,128)(2,1)S(1)} custom-call(s32[2,4]{1,0:T(2,128)S(1)} %copy-done.1, s32[5]{0:T(128)S(1)} %stack.19.place, bf16[8,320,320]{2,1,0:T(8,128)(2,1)} %bitcast.17, bf16[8,320,320]{2,1,0:T(8,128)(2,1)} %bitcast.18, bf16[8,320,320]{2,1,0:T(8,128)(2,1)} %bitcast.25, bf16[8,320,320]{2,1,0:T(8,128)(2,1)} %bitcast.26, ...), custom_call_target="tpu_custom_call" | custom-call | flops 1024 | bytes 1024 | tf_op jit(solution)/shard_map/local_map/pallas_call | solution.py:89
  17.6 12.2 %prepare.1 = (bf16[3040,128]{1,0:T(8,128)(2,1)S(1)}, bf16[4,320,1280]{2,1,0:T(8,128)(2,1)S(1)}, bf16[4,320,1600]{2,1,0:T(8,128)(2,1)S(1)}, f32[4,320,128]{2,1,0:...) custom-call(s32[2,4]{1,0:T(2,128)S(1)} %copy-done.1, ...), custom_call_target="tpu_custom_call" | custom-call | flops 1024 | bytes 1024 | tf_op jit(solution)/shard_map/prepare/pallas_call | solution.py:185
  29.7 13.6 %collective-permute-done.1.near = bf16[3040,128]{1,0:T(8,128)(2,1)S(1)} collective-permute-done((bf16[3040,128]{1,0:T(8,128)(2,1)S(1)}, bf16[3040,128]{1,0:T(8,128)(2,1)S(1)}, u32[]{:S(2)}, u32[]{:S(2)}) %collective-permute-start.1) | collective-permute-done | bytes 778272 | tf_op jit(solution)/shard_map/ppermute | solution.py:485
  43.3 3.9 %group_back.1 = (bf16[320,320]{1,0:T(8,128)(2,1)S(1)}, bf16[320,320]{1,0:T(8,128)(2,1)S(1)}, f32[320,128]{1,0:T(8,128)S(1)}, bf16[320,320]{1,0:T(8,128)(2,1)S(1)...) custom-call(s32[5]{0:T(128)S(1)} %stack.19.place, bf16[3040,128]{1,0:T(8,128)(2,1)S(1)} %collective-permute-done.across, ...), custom_call_target="tpu_custom_call" | custom-call | flops 1024 | bytes 1024 | tf_op jit(solution)/shard_map/group_back/pallas_call | solution.py:374
  49.8 5.5 %collective-permute-start.3 = (bf16[320,128]{1,0:T(8,128)(2,1)S(1)}, bf16[320,128]{1,0:T(8,128)(2,1)S(1)}, u32[]{:S(2)}, u32[]{:S(2)}) collective-permute-start(bf16[320,128]{1,0:T(8,128)(2,1)S(1)} %get-tuple-element.45), channel_id=1, source_target_pairs={{0,64},{16,80},{32,96},{48,112},{1,65},{17,81},{33,97},{49,113},{2... | collective-permute-start | bytes 245768 | tf_op jit(solution)/shard_map/ppermute | solution.py:482
  55.3 2.0 %collective-permute-done.3.incoming.hop1 = bf16[320,128]{1,0:T(8,128)(2,1)S(1)} collective-permute-done((bf16[320,128]{1,0:T(8,128)(2,1)S(1)}, bf16[320,128]{1,0:T(8,128)(2,1)S(1)}, u32[]{:S(2)}, u32[]{:S(2)}) %collective-permute-start.3) | collective-permute-done | bytes 81952 | tf_op jit(solution)/shard_map/ppermute | solution.py:482
  59.6 1.9 %entering.1 = (bf16[4,320,128]{2,1,0:T(8,128)(2,1)S(1)}, f32[4,320,128]{2,1,0:T(8,128)S(1)}, bf16[320,128]{1,0:T(8,128)(2,1)S(1)}, bf16[4,3040,128]{2,1,0:T(8,128)(2,1)S(1)}) custom-call(s32[5]{0:T(128)S(1)} %stack.19.place, bf16[3040,128]{1,0:T(8,128)(2,1)S(1)} %collective-permute-done.across, bf16[3040,128]{1,0:T(8,128)(2,1)S(1)} %collective-permute-done.1.near, ...), custom_call_target="tpu_custom_call" | custom-call | flops 1024 | bytes 1024 | tf_op jit(solution)/shard_map/entering/pallas_call | solution.py:374
  62.3 3.5 %collective-permute-done.5.far = bf16[1120,128]{1,0:T(8,128)(2,1)S(1)} collective-permute-done((bf16[1120,128]{1,0:T(8,128)(2,1)S(1)}, bf16[1120,128]{1,0:T(8,128)(2,1)S(1)}, u32[]{:S(2)}, u32[]{:S(2)}) %collective-permute-start.5) | collective-permute-done | bytes 286752 | tf_op jit(solution)/shard_map/ppermute | solution.py:482
  68.6 8.3 %collective-permute-done.9.hop_zero = bf16[320,128]{1,0:T(8,128)(2,1)S(1)} collective-permute-done((bf16[320,128]{1,0:T(8,128)(2,1)S(1)}, bf16[320,128]{1,0:T(8,128)(2,1)S(1)}, u32[]{:S(2)}, u32[]{:S(2)}) %collective-permute-start.9) | collective-permute-done | bytes 81952 | tf_op jit(solution)/shard_map/ppermute | solution.py:482
  76.9 1.6 %interfaces.1 = (bf16[640,128]{1,0:T(8,128)(2,1)S(1)}, bf16[640,128]{1,0:T(8,128)(2,1)S(1)}, bf16[640,128]{1,0:T(8,128)(2,1)S(1)}, bf16[640,128]{1,0:T(8,128)(2,1)S(1)}) custom-call(s32[5]{0:T(128)S(1)} %stack.19.place, bf16[4,3040,128]{2,1,0:T(8,128)(2,1)S(1)} %get-tuple-element.51.maps, bf16[1120,128]{1,0:T(8,128)(2,1)S(1)} %collective-permute-done.5.far, ...), custom_call_target="tpu_custom_call" | custom-call | flops 1024 | bytes 1024 | tf_op jit(solution)/shard_map/interfaces/pallas_call | solution.py:374
  78.5 2.4 %collective-permute-start.10 = (bf16[640,128]{1,0:T(8,128)(2,1)S(1)}, bf16[640,128]{1,0:T(8,128)(2,1)S(1)}, u32[]{:S(2)}, u32[]{:S(2)}) collective-permute-start(bf16[640,128]{1,0:T(8,128)(2,1)S(1)} %get-tuple-element.60), channel_id=1, source_target_pairs={{0,16},{16,0},{32,48},{48,32},{64,80},{80,64},{96,112},{112,96},{1... | collective-permute-start | bytes 491528 | tf_op jit(solution)/shard_map/ppermute | solution.py:485
  80.9 3.1 %collective-permute-start.11 = (bf16[640,128]{1,0:T(8,128)(2,1)S(1)}, bf16[640,128]{1,0:T(8,128)(2,1)S(1)}, u32[]{:S(2)}, u32[]{:S(2)}) collective-permute-start(bf16[640,128]{1,0:T(8,128)(2,1)S(1)} %get-tuple-element.61), channel_id=1, source_target_pairs={{0,32},{16,48},{32,0},{48,16},{64,96},{80,112},{96,64},{112,80},{1... | collective-permute-start | bytes 491528 | tf_op jit(solution)/shard_map/ppermute | solution.py:485
  85.4 2.9 %collective-permute-done.11.next_one = bf16[640,128]{1,0:T(8,128)(2,1)S(1)} collective-permute-done((bf16[640,128]{1,0:T(8,128)(2,1)S(1)}, bf16[640,128]{1,0:T(8,128)(2,1)S(1)}, u32[]{:S(2)}, u32[]{:S(2)}) %collective-permute-start.11) | collective-permute-done | bytes 163872 | tf_op jit(solution)/shard_map/ppermute | solution.py:485
  88.3 3.4 %collective-permute-done.12.across = bf16[640,128]{1,0:T(8,128)(2,1)S(1)} collective-permute-done((bf16[640,128]{1,0:T(8,128)(2,1)S(1)}, bf16[640,128]{1,0:T(8,128)(2,1)S(1)}, u32[]{:S(2)}, u32[]{:S(2)}) %collective-permute-start.12) | collective-permute-done | bytes 163872 | tf_op jit(solution)/shard_map/ppermute | solution.py:485
  91.7 1.6 %finish_second.1 = (bf16[4,320,128]{2,1,0:T(8,128)(2,1)S(1)}, bf16[4,320,128]{2,1,0:T(8,128)(2,1)S(1)}, bf16[4,320,128]{2,1,0:T(8,128)(2,1)S(1)}, bf16[4,320,128]{2,1,0:T(8,128)(2,1)S(1)}) custom-call(s32[5]{0:T(128)S(1)} %stack.19.place, bf16[640,128]{1,0:T(8,128)(2,1)S(1)} %collective-permute-done.10.near, ...), custom_call_target="tpu_custom_call" | custom-call | flops 1024 | bytes 1024 | tf_op jit(solution)/shard_map/finish_second/pallas_call | solution.py:374
  94.7 1.8 %finish_first.1 = (bf16[2,320,128]{2,1,0:T(8,128)(2,1)S(1)}, bf16[4,320,128]{2,1,0:T(8,128)(2,1)S(1)}) custom-call(s32[5]{0:T(128)S(1)} %stack.19.place, bf16[4,320,128]{2,1,0:T(8,128)(2,1)S(1)} %get-tuple-element.66.fronts, bf16[4,320,1600]{2,1,0:T(8,128)(2,1)S(1)} %get-tuple-element.67.second_ops, f32[4,320,128]{2,1,0:T(8,128)S(1)} %get-tuple-element.68.y0, ...), custom_call_target="tpu_custom_call" | custom-call | flops 1024 | bytes 1024 | tf_op jit(solution)/shard_map/finish_first/pallas_call | solution.py:374
  96.6 1.9 %collective-permute-start.13 = (bf16[2,320,128]{2,1,0:T(8,128)(2,1)S(1)}, bf16[2,320,128]{2,1,0:T(8,128)(2,1)S(1)}, u32[]{:S(2)}, u32[]{:S(2)}) collective-permute-start(bf16[2,320,128]{2,1,0:T(8,128)(2,1)S(1)} %get-tuple-element.74), channel_id=1, source_target_pairs={{1,2},{2,1},{3,4},{4,3},{5,6},{6,5},{7,8},{8,7},{9,10},{10,9},{11,... | collective-permute-start | bytes 491528 | tf_op jit(solution)/shard_map/ppermute | solution.py:551
  98.5 1.8 %first_rows.1 = (bf16[2,320,128]{2,1,0:T(8,128)(2,1)S(1)}, f32[2,2,320,128]{3,2,1,0:T(8,128)S(1)}) custom-call(s32[5]{0:T(128)S(1)} %stack.19.place, bf16[4,2,320,1600]{3,2,1,0:T(8,128)(2,1)S(1)} %get-tuple-element.41.rows, bf16[4,320,128]{2,1,0:T(8,128)(2,1)S(1)} %get-tuple-element.71.firsts, bf16[4,320,128]{2,1,0:T(8,128)(2,1)S(1)} %get-tuple-element.69.tops, ...), custom_call_target="tpu_custom_call" | custom-call | flops 1024 | bytes 1024 | tf_op jit(solution)/shard_map/first_rows/pallas_call | solution.py:374
  100.3 1.7 %collective-permute-start.15 = (bf16[2,320,128]{2,1,0:T(8,128)(2,1)S(1)}, bf16[2,320,128]{2,1,0:T(8,128)(2,1)S(1)}, u32[]{:S(2)}, u32[]{:S(2)}) collective-permute-start(bf16[2,320,128]{2,1,0:T(8,128)(2,1)S(1)} %get-tuple-element.75), channel_id=1, source_target_pairs={{0,1},{1,0},{2,3},{3,2},{4,5},{5,4},{6,7},{7,6},{8,9},{9,8},{10,11... | collective-permute-start | bytes 491528 | tf_op jit(solution)/shard_map/ppermute | solution.py:556
  102.0 2.6 %second_rows.1 = (bf16[8,320,128]{2,1,0:T(8,128)(2,1)}, f32[2,2,320,128]{3,2,1,0:T(8,128)S(1)}) custom-call(s32[2,4]{1,0:T(2,128)S(1)} %copy-done.1, bf16[4,2,320,1600]{3,2,1,0:T(8,128)(2,1)S(1)} %get-tuple-element.41.rows, bf16[4,320,128]{2,1,0:T(8,128)(2,1)S(1)} %get-tuple-element.71.firsts, bf16[4,320,128]{2,1,0:T(8,128)(2,1)S(1)} %get-tuple-element.69.tops, ...), custom_call_target="tpu_custom_call" | custom-call | flops 1024 | bytes 1024 | tf_op jit(solution)/shard_map/second_rows/pallas_call | solution.py:374
  105.3 2.1 %edge_jacobian.1 = bf16[8,320,128]{2,1,0:T(8,128)(2,1)} custom-call(s32[2,4]{1,0:T(2,128)S(1)} %copy-done.1, s32[5]{0:T(128)S(1)} %stack.19.place, bf16[2,320,128]{2,1,0:T(8,128)(2,1)S(1)} %collective-permute-done.13.beside, bf16[4,320,128]{2,1,0:T(8,128)(2,1)S(1)} %collective-permute-done.14.below, bf16[2,320,128]{2,1,0:T(8,128)(2,1)S(1)} %collective-permute-done.15.within, ...), custom_call_target="tpu_custom_call" | custom-call | flops 1024 | bytes 1024 | tf_op jit(solution)/shard_map/edge_jacobian/pallas_call | solution.py:374
  (28 shorter events, 14.3 us)
Async XLA Ops:
  0.7 0.7 copy-start
  1.4 7.4 %copy-start.1 = (s32[2,4]{1,0:T(2,128)S(1)}, s32[2,4]{1,0:T(2,128)}, u32[]{:S(2)}) copy-start(s32[2,4]{1,0:T(2,128)} %slots.11) | copy-start | bytes 100
  5.0 24.7 %collective-permute-start = (bf16[3040,128]{1,0:T(8,128)(2,1)S(1)}, bf16[3040,128]{1,0:T(8,128)(2,1)S(1)}, u32[]{:S(2)}, u32[]{:S(2)}) collective-permute-start(bf16[3040,128]{1,0:T(8,128)(2,1)S(1)} %local_map.3), channel_id=1, source_target_pairs={{0,48},{16,32},{32,16},{48,0},{64,112},{80,96},{96,80},{112,64},{1... | collective-permute-start | bytes 2334728 | tf_op jit(solution)/shard_map/ppermute | solution.py:485
  12.4 30.9 %collective-permute-start.1 = (bf16[3040,128]{1,0:T(8,128)(2,1)S(1)}, bf16[3040,128]{1,0:T(8,128)(2,1)S(1)}, u32[]{:S(2)}, u32[]{:S(2)}) collective-permute-start(bf16[3040,128]{1,0:T(8,128)(2,1)S(1)} %local_map.4), channel_id=1, source_target_pairs={{0,16},{16,0},{32,48},{48,32},{64,80},{80,64},{96,112},{112,96},{1... | collective-permute-start | bytes 2334728 | tf_op jit(solution)/shard_map/ppermute | solution.py:485
  17.4 25.9 %collective-permute-start.2 = (bf16[3040,128]{1,0:T(8,128)(2,1)S(1)}, bf16[3040,128]{1,0:T(8,128)(2,1)S(1)}, u32[]{:S(2)}, u32[]{:S(2)}) collective-permute-start(bf16[3040,128]{1,0:T(8,128)(2,1)S(1)} %local_map.5), channel_id=1, source_target_pairs={{0,32},{16,48},{32,0},{48,16},{64,96},{80,112},{96,64},{112,80},{1... | collective-permute-start | bytes 2334728 | tf_op jit(solution)/shard_map/ppermute | solution.py:485
  47.2 18.6 %collective-permute-start.5 = (bf16[1120,128]{1,0:T(8,128)(2,1)S(1)}, bf16[1120,128]{1,0:T(8,128)(2,1)S(1)}, u32[]{:S(2)}, u32[]{:S(2)}) collective-permute-start(bf16[1120,128]{1,0:T(8,128)(2,1)S(1)} %get-tuple-element.52), channel_id=1, source_target_pairs={{192,128},{208,144},{224,160},{240,176},{64,0},{80,16},{96,32},{11... | collective-permute-start | bytes 860168 | tf_op jit(solution)/shard_map/ppermute | solution.py:482
  49.8 7.5 %collective-permute-start.3 = (bf16[320,128]{1,0:T(8,128)(2,1)S(1)}, bf16[320,128]{1,0:T(8,128)(2,1)S(1)}, u32[]{:S(2)}, u32[]{:S(2)}) collective-permute-start(bf16[320,128]{1,0:T(8,128)(2,1)S(1)} %get-tuple-element.45), channel_id=1, source_target_pairs={{0,64},{16,80},{32,96},{48,112},{1,65},{17,81},{33,97},{49,113},{2... | collective-permute-start | bytes 245768 | tf_op jit(solution)/shard_map/ppermute | solution.py:482
  57.6 2.0 %collective-permute-start.4 = (bf16[320,128]{1,0:T(8,128)(2,1)S(1)}, bf16[320,128]{1,0:T(8,128)(2,1)S(1)}, u32[]{:S(2)}, u32[]{:S(2)}) collective-permute-start(bf16[320,128]{1,0:T(8,128)(2,1)S(1)} %get-tuple-element.50), channel_id=1, source_target_pairs={{64,128},{80,144},{96,160},{112,176},{65,129},{81,145},{97,161},{1... | collective-permute-start | bytes 245768 | tf_op jit(solution)/shard_map/ppermute | solution.py:482
  58.2 10.4 %collective-permute-start.6 = (bf16[320,128]{1,0:T(8,128)(2,1)S(1)}, bf16[320,128]{1,0:T(8,128)(2,1)S(1)}, u32[]{:S(2)}, u32[]{:S(2)}) collective-permute-start(bf16[320,128]{1,0:T(8,128)(2,1)S(1)} %get-tuple-element.53), channel_id=1, source_target_pairs={{64,0},{80,16},{96,32},{112,48},{65,1},{81,17},{97,33},{113,49},{6... | collective-permute-start | bytes 245768 | tf_op jit(solution)/shard_map/ppermute | solution.py:482
  61.5 7.2 %collective-permute-start.7 = (bf16[320,128]{1,0:T(8,128)(2,1)S(1)}, bf16[320,128]{1,0:T(8,128)(2,1)S(1)}, u32[]{:S(2)}, u32[]{:S(2)}) collective-permute-start(bf16[320,128]{1,0:T(8,128)(2,1)S(1)} %get-tuple-element.54), channel_id=1, source_target_pairs={{128,192},{144,208},{160,224},{176,240},{129,193},{145,209},{161,2... | collective-permute-start | bytes 245768 | tf_op jit(solution)/shard_map/ppermute | solution.py:482
  66.6 10.2 %collective-permute-start.9 = (bf16[320,128]{1,0:T(8,128)(2,1)S(1)}, bf16[320,128]{1,0:T(8,128)(2,1)S(1)}, u32[]{:S(2)}, u32[]{:S(2)}) collective-permute-start(bf16[320,128]{1,0:T(8,128)(2,1)S(1)} %get-tuple-element.56), channel_id=1, source_target_pairs={{128,0},{144,16},{160,32},{176,48},{129,1},{145,17},{161,33},{177,... | collective-permute-start | bytes 245768 | tf_op jit(solution)/shard_map/ppermute | solution.py:482
  67.9 8.9 %collective-permute-start.8 = (bf16[320,128]{1,0:T(8,128)(2,1)S(1)}, bf16[320,128]{1,0:T(8,128)(2,1)S(1)}, u32[]{:S(2)}, u32[]{:S(2)}) collective-permute-start(bf16[320,128]{1,0:T(8,128)(2,1)S(1)} %get-tuple-element.56), channel_id=1, source_target_pairs={{128,64},{144,80},{160,96},{176,112},{129,65},{145,81},{161,97},{1... | collective-permute-start | bytes 245768 | tf_op jit(solution)/shard_map/ppermute | solution.py:482
  78.5 6.9 %collective-permute-start.10 = (bf16[640,128]{1,0:T(8,128)(2,1)S(1)}, bf16[640,128]{1,0:T(8,128)(2,1)S(1)}, u32[]{:S(2)}, u32[]{:S(2)}) collective-permute-start(bf16[640,128]{1,0:T(8,128)(2,1)S(1)} %get-tuple-element.60), channel_id=1, source_target_pairs={{0,16},{16,0},{32,48},{48,32},{64,80},{80,64},{96,112},{112,96},{1... | collective-permute-start | bytes 491528 | tf_op jit(solution)/shard_map/ppermute | solution.py:485
  80.9 7.4 %collective-permute-start.11 = (bf16[640,128]{1,0:T(8,128)(2,1)S(1)}, bf16[640,128]{1,0:T(8,128)(2,1)S(1)}, u32[]{:S(2)}, u32[]{:S(2)}) collective-permute-start(bf16[640,128]{1,0:T(8,128)(2,1)S(1)} %get-tuple-element.61), channel_id=1, source_target_pairs={{0,32},{16,48},{32,0},{48,16},{64,96},{80,112},{96,64},{112,80},{1... | collective-permute-start | bytes 491528 | tf_op jit(solution)/shard_map/ppermute | solution.py:485
  84.0 7.7 %collective-permute-start.12 = (bf16[640,128]{1,0:T(8,128)(2,1)S(1)}, bf16[640,128]{1,0:T(8,128)(2,1)S(1)}, u32[]{:S(2)}, u32[]{:S(2)}) collective-permute-start(bf16[640,128]{1,0:T(8,128)(2,1)S(1)} %get-tuple-element.62), channel_id=1, source_target_pairs={{0,48},{16,32},{32,16},{48,0},{64,112},{80,96},{96,80},{112,64},{1... | collective-permute-start | bytes 491528 | tf_op jit(solution)/shard_map/ppermute | solution.py:485
  93.3 12.0 %collective-permute-start.14 = (bf16[4,320,128]{2,1,0:T(8,128)(2,1)S(1)}, bf16[4,320,128]{2,1,0:T(8,128)(2,1)S(1)}, u32[]{:S(2)}, u32[]{:S(2)}) collective-permute-start(bf16[4,320,128]{2,1,0:T(8,128)(2,1)S(1)} %get-tuple-element.69.tops), channel_id=1, source_target_pairs={{0,16},{16,32},{32,48},{48,64},{64,80},{80,96},{96,112},{112,128},... | collective-permute-start | bytes 983048 | tf_op jit(solution)/shard_map/ppermute | solution.py:543
  96.6 8.7 %collective-permute-start.13 = (bf16[2,320,128]{2,1,0:T(8,128)(2,1)S(1)}, bf16[2,320,128]{2,1,0:T(8,128)(2,1)S(1)}, u32[]{:S(2)}, u32[]{:S(2)}) collective-permute-start(bf16[2,320,128]{2,1,0:T(8,128)(2,1)S(1)} %get-tuple-element.74), channel_id=1, source_target_pairs={{1,2},{2,1},{3,4},{4,3},{5,6},{6,5},{7,8},{8,7},{9,10},{10,9},{11,... | collective-permute-start | bytes 491528 | tf_op jit(solution)/shard_map/ppermute | solution.py:551
  100.3 5.0 %collective-permute-start.15 = (bf16[2,320,128]{2,1,0:T(8,128)(2,1)S(1)}, bf16[2,320,128]{2,1,0:T(8,128)(2,1)S(1)}, u32[]{:S(2)}, u32[]{:S(2)}) collective-permute-start(bf16[2,320,128]{2,1,0:T(8,128)(2,1)S(1)} %get-tuple-element.75), channel_id=1, source_target_pairs={{0,1},{1,0},{2,3},{3,2},{4,5},{5,4},{6,7},{7,6},{8,9},{9,8},{10,11... | collective-permute-start | bytes 491528 | tf_op jit(solution)/shard_map/ppermute | solution.py:556
where the time goes:
time: 109 us; the launch traced here: 107 us
  Pallas kernels  42.7 us (39%)
  waiting for transfers between devices  35 us (32%)
  starting transfers between devices  28 us (26%)
    ppermute x6, waiting for transfers between devices, to_peer(): lax.ppermute(values, 'sweep', [(i, i ^ distance) for i in range(count)])  20.6 us
    pallas_call x11, Pallas kernels, whole_call(): pl.pallas_call(kernel, in_specs=specs, out_specs=[pl.BlockSpec(memory_spa...  19.7 us
    ppermute x7, waiting for transfers between devices, hop(): return lax.ppermute(values, 'sweep', pairs)  13.8 us
    pallas_call x1, Pallas kernels, prepare(): pl.pallas_call(prepare_kernel, grid_spec=pltpu.PrefetchScalarGridSpec(num...  12.2 us
    ppermute x7, starting transfers between devices, hop(): return lax.ppermute(values, 'sweep', pairs)  11.6 us
    ppermute x6, starting transfers between devices, to_peer(): lax.ppermute(values, 'sweep', [(i, i ^ distance) for i in range(count)])  11.4 us
    pallas_call x3, Pallas kernels, element_call(): pl.pallas_call(kernel, grid_spec=pltpu.PrefetchScalarGridSpec(num_scalar_...  10.9 us
  transfers between devices with their start and end apart: 16, of which 8 were waited for; matrix products, arithmetic and copies ran while one was open for 0% of the time, Pallas kernels for 28%

commit v1 on v0

--- a/solution.py
+++ b/solution.py
@@ -398,16 +398,13 @@
         tops[p], rests[p] = halves(x1)
 
 
-def finish_first_kernel(place, fronts, second_ops, y0, tops, rests, beside, firsts):
+def finish_first_kernel(fronts, second_ops, y0, tops, rests, firsts):
     n = y0.shape[1]
     for p in range(GROUP):
         front = fronts[p]
         top = tops[p]
         around = jnp.concatenate([front, front, top, top, rests[p]], axis=0)
         firsts[p] = (y0[p] + mm(second_ops[p], around)).astype(BF)
-    even = lax.rem(place[1], 2) == 0
-    for s, values in enumerate((firsts, tops)):
-        beside[s] = jnp.where(even, values[0], values[GROUP - 1])
 
 
 def row_products(chosen, rows, firsts, tops, backs, partial):
@@ -425,11 +422,12 @@
             partial[i, s] = mm(rows[p, s], jnp.concatenate(around, axis=0))
 
 
-def first_rows_kernel(place, rows, firsts, tops, backs, within, partial):
+def first_rows_kernel(place, rows, firsts, tops, backs, beside, within, partial):
     even = lax.rem(place[1], 2) == 0
     row_products((0, 1), rows, firsts, tops, backs, partial)
     for s, values in enumerate((firsts, tops)):
         within[s] = jnp.where(even, values[GROUP - 1], values[0])
+        beside[s] = jnp.where(even, values[0], values[GROUP - 1])
 
 
 def second_rows_kernel(slots, rows, firsts, tops, backs, precond, partial):
@@ -541,18 +539,18 @@
         finish_second_kernel, [four] * 4, [place], *ends, first_ops, c_own, name="finish_second"
     )
     below = lax.ppermute(tops, "sweep", [(i, (i + 1) % count) for i in range(count)])
-    beside, firsts = whole_call(
-        finish_first_kernel, [pair, four], [place],
+    (firsts,) = whole_call(
+        finish_first_kernel, [four], [],
         fronts, second_ops, y_own, tops, rests, name="finish_first",
+    )
+    part = ((2, 2, n, cols), F32)
+    beside, within, partial_a = whole_call(
+        first_rows_kernel, [pair, pair, part], [place], rows, firsts, tops, backs, name="first_rows"
     )
     aside = []
     for i in range(1, across - 1, 2):
         aside += [(i, i + 1), (i + 1, i)]
     beside = lax.ppermute(beside, "cross", aside)
-    part = ((2, 2, n, cols), F32)
-    within, partial_a = whole_call(
-        first_rows_kernel, [pair, part], [place], rows, firsts, tops, backs, name="first_rows"
-    )
     within = lax.ppermute(within, "cross", [(i, i ^ 1) for i in range(across)])
     every = ((2 * GROUP, n, cols), BF)
     precond, partial_b = whole_call(

time: 109 us -> 110 us (level)
  waiting for transfers between devices: 35 us -> 36.9 us
    ppermute x1, waiting for transfers between devices: 0.67 us -> 2.49 us  [local(): beside = lax.ppermute(beside, 'cross', aside)]
  transfers between devices with their start and end apart: 16 -> 16, of which waited for: 8 -> 8; matrix products, arithmetic and copies ran while one was open for 0% -> 0% of each run, Pallas kernels for 28% -> 27%
where the time goes in v1:
time: 110 us; the launch traced here: 109 us
  Pallas kernels  42.2 us (38%)
  waiting for transfers between devices  36.9 us (34%)
  starting transfers between devices  28 us (25%)
    ppermute x6, waiting for transfers between devices, to_peer(): lax.ppermute(values, 'sweep', [(i, i ^ distance) for i in range(count)])  20.6 us
    pallas_call x11, Pallas kernels, whole_call(): pl.pallas_call(kernel, in_specs=specs, out_specs=[pl.BlockSpec(memory_spa...  19.1 us
    ppermute x7, waiting for transfers between devices, hop(): return lax.ppermute(values, 'sweep', pairs)  13.8 us
    pallas_call x1, Pallas kernels, prepare(): pl.pallas_call(prepare_kernel, grid_spec=pltpu.PrefetchScalarGridSpec(num...  12.2 us
    ppermute x7, starting transfers between devices, hop(): return lax.ppermute(values, 'sweep', pairs)  11.6 us
    ppermute x6, starting transfers between devices, to_peer(): lax.ppermute(values, 'sweep', [(i, i ^ distance) for i in range(count)])  11.4 us
    pallas_call x3, Pallas kernels, element_call(): pl.pallas_call(kernel, grid_spec=pltpu.PrefetchScalarGridSpec(num_scalar_...  10.9 us
    ppermute x1, waiting for transfers between devices, local(): beside = lax.ppermute(beside, 'cross', aside)  2.49 us
  transfers between devices with their start and end apart: 16, of which 8 were waited for; matrix products, arithmetic and copies ran while one was open for 0% of the time, Pallas kernels for 27%

profile of v1, /device:TPU:8, one launch (start us, length us, event | category | flops | bytes accessed | tf_op | source)
XLA Modules:
  0.0 108.6 jit_solution(9426201558075466831)
XLA Ops:
  1.4 3.6 %local_map.3 = bf16[3040,128]{1,0:T(8,128)(2,1)S(1)} custom-call(s32[2,4]{1,0:T(2,128)S(1)} %copy-done, s32[5]{0:T(128)S(1)} %stack.19.place, bf16[8,320,320]{2,1,0:T(8,128)(2,1)} %bitcast.13, bf16[8,320,320]{2,1,0:T(8,128)(2,1)} %bitcast.14, bf16[8,320,320]{2,1,0:T(8,128)(2,1)} %bitcast.21, bf16[8,320,320]{2,1,0:T(8,128)(2,1)} %bitcast.22, ...), custom_call_target="tpu_custom_call" | custom-call | flops 1024 | bytes 1024 | tf_op jit(solution)/shard_map/local_map/pallas_call | solution.py:89
  5.0 3.7 %collective-permute-start = (bf16[3040,128]{1,0:T(8,128)(2,1)S(1)}, bf16[3040,128]{1,0:T(8,128)(2,1)S(1)}, u32[]{:S(2)}, u32[]{:S(2)}) collective-permute-start(bf16[3040,128]{1,0:T(8,128)(2,1)S(1)} %local_map.3), channel_id=1, source_target_pairs={{0,48},{16,32},{32,16},{48,0},{64,112},{80,96},{96,80},{112,64},{1... | collective-permute-start | bytes 2334728 | tf_op jit(solution)/shard_map/ppermute | solution.py:483
  8.8 3.6 %local_map.4 = bf16[3040,128]{1,0:T(8,128)(2,1)S(1)} custom-call(s32[2,4]{1,0:T(2,128)S(1)} %copy-done.1, s32[5]{0:T(128)S(1)} %stack.19.place, bf16[8,320,320]{2,1,0:T(8,128)(2,1)} %bitcast.15, bf16[8,320,320]{2,1,0:T(8,128)(2,1)} %bitcast.16, bf16[8,320,320]{2,1,0:T(8,128)(2,1)} %bitcast.23, bf16[8,320,320]{2,1,0:T(8,128)(2,1)} %bitcast.24, ...), custom_call_target="tpu_custom_call" | custom-call | flops 1024 | bytes 1024 | tf_op jit(solution)/shard_map/local_map/pallas_call | solution.py:89
  13.7 3.6 %local_map.5 = bf16[3040,128]{1,0:T(8,128)(2,1)S(1)} custom-call(s32[2,4]{1,0:T(2,128)S(1)} %copy-done.1, s32[5]{0:T(128)S(1)} %stack.19.place, bf16[8,320,320]{2,1,0:T(8,128)(2,1)} %bitcast.17, bf16[8,320,320]{2,1,0:T(8,128)(2,1)} %bitcast.18, bf16[8,320,320]{2,1,0:T(8,128)(2,1)} %bitcast.25, bf16[8,320,320]{2,1,0:T(8,128)(2,1)} %bitcast.26, ...), custom_call_target="tpu_custom_call" | custom-call | flops 1024 | bytes 1024 | tf_op jit(solution)/shard_map/local_map/pallas_call | solution.py:89
  17.6 12.2 %prepare.1 = (bf16[3040,128]{1,0:T(8,128)(2,1)S(1)}, bf16[4,320,1280]{2,1,0:T(8,128)(2,1)S(1)}, bf16[4,320,1600]{2,1,0:T(8,128)(2,1)S(1)}, f32[4,320,128]{2,1,0:...) custom-call(s32[2,4]{1,0:T(2,128)S(1)} %copy-done.1, ...), custom_call_target="tpu_custom_call" | custom-call | flops 1024 | bytes 1024 | tf_op jit(solution)/shard_map/prepare/pallas_call | solution.py:185
  29.7 13.6 %collective-permute-done.1.near = bf16[3040,128]{1,0:T(8,128)(2,1)S(1)} collective-permute-done((bf16[3040,128]{1,0:T(8,128)(2,1)S(1)}, bf16[3040,128]{1,0:T(8,128)(2,1)S(1)}, u32[]{:S(2)}, u32[]{:S(2)}) %collective-permute-start.1) | collective-permute-done | bytes 778272 | tf_op jit(solution)/shard_map/ppermute | solution.py:483
  43.3 3.9 %group_back.1 = (bf16[320,320]{1,0:T(8,128)(2,1)S(1)}, bf16[320,320]{1,0:T(8,128)(2,1)S(1)}, f32[320,128]{1,0:T(8,128)S(1)}, bf16[320,320]{1,0:T(8,128)(2,1)S(1)...) custom-call(s32[5]{0:T(128)S(1)} %stack.19.place, bf16[3040,128]{1,0:T(8,128)(2,1)S(1)} %collective-permute-done.across, ...), custom_call_target="tpu_custom_call" | custom-call | flops 1024 | bytes 1024 | tf_op jit(solution)/shard_map/group_back/pallas_call | solution.py:374
  49.8 5.5 %collective-permute-start.3 = (bf16[320,128]{1,0:T(8,128)(2,1)S(1)}, bf16[320,128]{1,0:T(8,128)(2,1)S(1)}, u32[]{:S(2)}, u32[]{:S(2)}) collective-permute-start(bf16[320,128]{1,0:T(8,128)(2,1)S(1)} %get-tuple-element.44), channel_id=1, source_target_pairs={{0,64},{16,80},{32,96},{48,112},{1,65},{17,81},{33,97},{49,113},{2... | collective-permute-start | bytes 245768 | tf_op jit(solution)/shard_map/ppermute | solution.py:480
  55.3 2.0 %collective-permute-done.3.incoming.hop1 = bf16[320,128]{1,0:T(8,128)(2,1)S(1)} collective-permute-done((bf16[320,128]{1,0:T(8,128)(2,1)S(1)}, bf16[320,128]{1,0:T(8,128)(2,1)S(1)}, u32[]{:S(2)}, u32[]{:S(2)}) %collective-permute-start.3) | collective-permute-done | bytes 81952 | tf_op jit(solution)/shard_map/ppermute | solution.py:480
  59.6 1.9 %entering.1 = (bf16[4,320,128]{2,1,0:T(8,128)(2,1)S(1)}, f32[4,320,128]{2,1,0:T(8,128)S(1)}, bf16[320,128]{1,0:T(8,128)(2,1)S(1)}, bf16[4,3040,128]{2,1,0:T(8,128)(2,1)S(1)}) custom-call(s32[5]{0:T(128)S(1)} %stack.19.place, bf16[3040,128]{1,0:T(8,128)(2,1)S(1)} %collective-permute-done.across, bf16[3040,128]{1,0:T(8,128)(2,1)S(1)} %collective-permute-done.1.near, ...), custom_call_target="tpu_custom_call" | custom-call | flops 1024 | bytes 1024 | tf_op jit(solution)/shard_map/entering/pallas_call | solution.py:374
  62.3 3.5 %collective-permute-done.5.far = bf16[1120,128]{1,0:T(8,128)(2,1)S(1)} collective-permute-done((bf16[1120,128]{1,0:T(8,128)(2,1)S(1)}, bf16[1120,128]{1,0:T(8,128)(2,1)S(1)}, u32[]{:S(2)}, u32[]{:S(2)}) %collective-permute-start.5) | collective-permute-done | bytes 286752 | tf_op jit(solution)/shard_map/ppermute | solution.py:480
  68.6 8.3 %collective-permute-done.9.hop_zero = bf16[320,128]{1,0:T(8,128)(2,1)S(1)} collective-permute-done((bf16[320,128]{1,0:T(8,128)(2,1)S(1)}, bf16[320,128]{1,0:T(8,128)(2,1)S(1)}, u32[]{:S(2)}, u32[]{:S(2)}) %collective-permute-start.9) | collective-permute-done | bytes 81952 | tf_op jit(solution)/shard_map/ppermute | solution.py:480
  76.9 1.6 %interfaces.1 = (bf16[640,128]{1,0:T(8,128)(2,1)S(1)}, bf16[640,128]{1,0:T(8,128)(2,1)S(1)}, bf16[640,128]{1,0:T(8,128)(2,1)S(1)}, bf16[640,128]{1,0:T(8,128)(2,1)S(1)}) custom-call(s32[5]{0:T(128)S(1)} %stack.19.place, bf16[4,3040,128]{2,1,0:T(8,128)(2,1)S(1)} %get-tuple-element.50.maps, bf16[1120,128]{1,0:T(8,128)(2,1)S(1)} %collective-permute-done.5.far, ...), custom_call_target="tpu_custom_call" | custom-call | flops 1024 | bytes 1024 | tf_op jit(solution)/shard_map/interfaces/pallas_call | solution.py:374
  78.5 2.4 %collective-permute-start.10 = (bf16[640,128]{1,0:T(8,128)(2,1)S(1)}, bf16[640,128]{1,0:T(8,128)(2,1)S(1)}, u32[]{:S(2)}, u32[]{:S(2)}) collective-permute-start(bf16[640,128]{1,0:T(8,128)(2,1)S(1)} %get-tuple-element.59), channel_id=1, source_target_pairs={{0,16},{16,0},{32,48},{48,32},{64,80},{80,64},{96,112},{112,96},{1... | collective-permute-start | bytes 491528 | tf_op jit(solution)/shard_map/ppermute | solution.py:483
  80.9 3.1 %collective-permute-start.11 = (bf16[640,128]{1,0:T(8,128)(2,1)S(1)}, bf16[640,128]{1,0:T(8,128)(2,1)S(1)}, u32[]{:S(2)}, u32[]{:S(2)}) collective-permute-start(bf16[640,128]{1,0:T(8,128)(2,1)S(1)} %get-tuple-element.60), channel_id=1, source_target_pairs={{0,32},{16,48},{32,0},{48,16},{64,96},{80,112},{96,64},{112,80},{1... | collective-permute-start | bytes 491528 | tf_op jit(solution)/shard_map/ppermute | solution.py:483
  85.4 2.9 %collective-permute-done.11.next_one = bf16[640,128]{1,0:T(8,128)(2,1)S(1)} collective-permute-done((bf16[640,128]{1,0:T(8,128)(2,1)S(1)}, bf16[640,128]{1,0:T(8,128)(2,1)S(1)}, u32[]{:S(2)}, u32[]{:S(2)}) %collective-permute-start.11) | collective-permute-done | bytes 163872 | tf_op jit(solution)/shard_map/ppermute | solution.py:483
  88.3 3.4 %collective-permute-done.12.across = bf16[640,128]{1,0:T(8,128)(2,1)S(1)} collective-permute-done((bf16[640,128]{1,0:T(8,128)(2,1)S(1)}, bf16[640,128]{1,0:T(8,128)(2,1)S(1)}, u32[]{:S(2)}, u32[]{:S(2)}) %collective-permute-start.12) | collective-permute-done | bytes 163872 | tf_op jit(solution)/shard_map/ppermute | solution.py:483
  91.7 1.6 %finish_second.1 = (bf16[4,320,128]{2,1,0:T(8,128)(2,1)S(1)}, bf16[4,320,128]{2,1,0:T(8,128)(2,1)S(1)}, bf16[4,320,128]{2,1,0:T(8,128)(2,1)S(1)}, bf16[4,320,128]{2,1,0:T(8,128)(2,1)S(1)}) custom-call(s32[5]{0:T(128)S(1)} %stack.19.place, bf16[640,128]{1,0:T(8,128)(2,1)S(1)} %collective-permute-done.10.near, ...), custom_call_target="tpu_custom_call" | custom-call | flops 1024 | bytes 1024 | tf_op jit(solution)/shard_map/finish_second/pallas_call | solution.py:374
  96.0 1.8 %first_rows.1 = (bf16[2,320,128]{2,1,0:T(8,128)(2,1)S(1)}, bf16[2,320,128]{2,1,0:T(8,128)(2,1)S(1)}, f32[2,2,320,128]{3,2,1,0:T(8,128)S(1)}) custom-call(s32[5]{0:T(128)S(1)} %stack.19.place, bf16[4,2,320,1600]{3,2,1,0:T(8,128)(2,1)S(1)} %get-tuple-element.40.rows, bf16[4,320,128]{2,1,0:T(8,128)(2,1)S(1)} %finish_first.1.firsts, ...), custom_call_target="tpu_custom_call" | custom-call | flops 1024 | bytes 1024 | tf_op jit(solution)/shard_map/first_rows/pallas_call | solution.py:374
  97.8 1.9 %collective-permute-start.13 = (bf16[2,320,128]{2,1,0:T(8,128)(2,1)S(1)}, bf16[2,320,128]{2,1,0:T(8,128)(2,1)S(1)}, u32[]{:S(2)}, u32[]{:S(2)}) collective-permute-start(bf16[2,320,128]{2,1,0:T(8,128)(2,1)S(1)} %get-tuple-element.72), channel_id=1, source_target_pairs={{1,2},{2,1},{3,4},{4,3},{5,6},{6,5},{7,8},{8,7},{9,10},{10,9},{11,... | collective-permute-start | bytes 491528 | tf_op jit(solution)/shard_map/ppermute | solution.py:553
  99.7 1.7 %collective-permute-start.15 = (bf16[2,320,128]{2,1,0:T(8,128)(2,1)S(1)}, bf16[2,320,128]{2,1,0:T(8,128)(2,1)S(1)}, u32[]{:S(2)}, u32[]{:S(2)}) collective-permute-start(bf16[2,320,128]{2,1,0:T(8,128)(2,1)S(1)} %get-tuple-element.73), channel_id=1, source_target_pairs={{0,1},{1,0},{2,3},{3,2},{4,5},{5,4},{6,7},{7,6},{8,9},{9,8},{10,11... | collective-permute-start | bytes 491528 | tf_op jit(solution)/shard_map/ppermute | solution.py:554
  101.5 2.6 %second_rows.1 = (bf16[8,320,128]{2,1,0:T(8,128)(2,1)}, f32[2,2,320,128]{3,2,1,0:T(8,128)S(1)}) custom-call(s32[2,4]{1,0:T(2,128)S(1)} %copy-done.1, bf16[4,2,320,1600]{3,2,1,0:T(8,128)(2,1)S(1)} %get-tuple-element.40.rows, bf16[4,320,128]{2,1,0:T(8,128)(2,1)S(1)} %finish_first.1.firsts, bf16[4,320,128]{2,1,0:T(8,128)(2,1)S(1)} %get-tuple-element.68.tops, ...), custom_call_target="tpu_custom_call" | custom-call | flops 1024 | bytes 1024 | tf_op jit(solution)/shard_map/second_rows/pallas_call | solution.py:374
  104.1 2.5 %collective-permute-done.13.beside = bf16[2,320,128]{2,1,0:T(8,128)(2,1)S(1)} collective-permute-done((bf16[2,320,128]{2,1,0:T(8,128)(2,1)S(1)}, bf16[2,320,128]{2,1,0:T(8,128)(2,1)S(1)}, u32[]{:S(2)}, u32[]{:S(2)}) %collective-permute-start.13) | collective-permute-done | bytes 163872 | tf_op jit(solution)/shard_map/ppermute | solution.py:553
  106.6 2.1 %edge_jacobian.1 = bf16[8,320,128]{2,1,0:T(8,128)(2,1)} custom-call(s32[2,4]{1,0:T(2,128)S(1)} %copy-done.1, s32[5]{0:T(128)S(1)} %stack.19.place, bf16[2,320,128]{2,1,0:T(8,128)(2,1)S(1)} %collective-permute-done.13.beside, bf16[4,320,128]{2,1,0:T(8,128)(2,1)S(1)} %collective-permute-done.14.below, bf16[2,320,128]{2,1,0:T(8,128)(2,1)S(1)} %collective-permute-done.15.within, ...), custom_call_target="tpu_custom_call" | custom-call | flops 1024 | bytes 1024 | tf_op jit(solution)/shard_map/edge_jacobian/pallas_call | solution.py:374
  (28 shorter events, 14.8 us)
Async XLA Ops:
  0.7 0.7 copy-start
  1.4 7.4 %copy-start.1 = (s32[2,4]{1,0:T(2,128)S(1)}, s32[2,4]{1,0:T(2,128)}, u32[]{:S(2)}) copy-start(s32[2,4]{1,0:T(2,128)} %slots.11) | copy-start | bytes 100
  5.0 24.7 %collective-permute-start = (bf16[3040,128]{1,0:T(8,128)(2,1)S(1)}, bf16[3040,128]{1,0:T(8,128)(2,1)S(1)}, u32[]{:S(2)}, u32[]{:S(2)}) collective-permute-start(bf16[3040,128]{1,0:T(8,128)(2,1)S(1)} %local_map.3), channel_id=1, source_target_pairs={{0,48},{16,32},{32,16},{48,0},{64,112},{80,96},{96,80},{112,64},{1... | collective-permute-start | bytes 2334728 | tf_op jit(solution)/shard_map/ppermute | solution.py:483
  12.4 30.9 %collective-permute-start.1 = (bf16[3040,128]{1,0:T(8,128)(2,1)S(1)}, bf16[3040,128]{1,0:T(8,128)(2,1)S(1)}, u32[]{:S(2)}, u32[]{:S(2)}) collective-permute-start(bf16[3040,128]{1,0:T(8,128)(2,1)S(1)} %local_map.4), channel_id=1, source_target_pairs={{0,16},{16,0},{32,48},{48,32},{64,80},{80,64},{96,112},{112,96},{1... | collective-permute-start | bytes 2334728 | tf_op jit(solution)/shard_map/ppermute | solution.py:483
  17.4 25.9 %collective-permute-start.2 = (bf16[3040,128]{1,0:T(8,128)(2,1)S(1)}, bf16[3040,128]{1,0:T(8,128)(2,1)S(1)}, u32[]{:S(2)}, u32[]{:S(2)}) collective-permute-start(bf16[3040,128]{1,0:T(8,128)(2,1)S(1)} %local_map.5), channel_id=1, source_target_pairs={{0,32},{16,48},{32,0},{48,16},{64,96},{80,112},{96,64},{112,80},{1... | collective-permute-start | bytes 2334728 | tf_op jit(solution)/shard_map/ppermute | solution.py:483
  47.2 18.6 %collective-permute-start.5 = (bf16[1120,128]{1,0:T(8,128)(2,1)S(1)}, bf16[1120,128]{1,0:T(8,128)(2,1)S(1)}, u32[]{:S(2)}, u32[]{:S(2)}) collective-permute-start(bf16[1120,128]{1,0:T(8,128)(2,1)S(1)} %get-tuple-element.51), channel_id=1, source_target_pairs={{192,128},{208,144},{224,160},{240,176},{64,0},{80,16},{96,32},{11... | collective-permute-start | bytes 860168 | tf_op jit(solution)/shard_map/ppermute | solution.py:480
  49.8 7.5 %collective-permute-start.3 = (bf16[320,128]{1,0:T(8,128)(2,1)S(1)}, bf16[320,128]{1,0:T(8,128)(2,1)S(1)}, u32[]{:S(2)}, u32[]{:S(2)}) collective-permute-start(bf16[320,128]{1,0:T(8,128)(2,1)S(1)} %get-tuple-element.44), channel_id=1, source_target_pairs={{0,64},{16,80},{32,96},{48,112},{1,65},{17,81},{33,97},{49,113},{2... | collective-permute-start | bytes 245768 | tf_op jit(solution)/shard_map/ppermute | solution.py:480
  57.6 2.0 %collective-permute-start.4 = (bf16[320,128]{1,0:T(8,128)(2,1)S(1)}, bf16[320,128]{1,0:T(8,128)(2,1)S(1)}, u32[]{:S(2)}, u32[]{:S(2)}) collective-permute-start(bf16[320,128]{1,0:T(8,128)(2,1)S(1)} %get-tuple-element.49), channel_id=1, source_target_pairs={{64,128},{80,144},{96,160},{112,176},{65,129},{81,145},{97,161},{1... | collective-permute-start | bytes 245768 | tf_op jit(solution)/shard_map/ppermute | solution.py:480
  58.2 10.4 %collective-permute-start.6 = (bf16[320,128]{1,0:T(8,128)(2,1)S(1)}, bf16[320,128]{1,0:T(8,128)(2,1)S(1)}, u32[]{:S(2)}, u32[]{:S(2)}) collective-permute-start(bf16[320,128]{1,0:T(8,128)(2,1)S(1)} %get-tuple-element.52), channel_id=1, source_target_pairs={{64,0},{80,16},{96,32},{112,48},{65,1},{81,17},{97,33},{113,49},{6... | collective-permute-start | bytes 245768 | tf_op jit(solution)/shard_map/ppermute | solution.py:480
  61.5 7.2 %collective-permute-start.7 = (bf16[320,128]{1,0:T(8,128)(2,1)S(1)}, bf16[320,128]{1,0:T(8,128)(2,1)S(1)}, u32[]{:S(2)}, u32[]{:S(2)}) collective-permute-start(bf16[320,128]{1,0:T(8,128)(2,1)S(1)} %get-tuple-element.53), channel_id=1, source_target_pairs={{128,192},{144,208},{160,224},{176,240},{129,193},{145,209},{161,2... | collective-permute-start | bytes 245768 | tf_op jit(solution)/shard_map/ppermute | solution.py:480
  66.6 10.2 %collective-permute-start.9 = (bf16[320,128]{1,0:T(8,128)(2,1)S(1)}, bf16[320,128]{1,0:T(8,128)(2,1)S(1)}, u32[]{:S(2)}, u32[]{:S(2)}) collective-permute-start(bf16[320,128]{1,0:T(8,128)(2,1)S(1)} %get-tuple-element.55), channel_id=1, source_target_pairs={{128,0},{144,16},{160,32},{176,48},{129,1},{145,17},{161,33},{177,... | collective-permute-start | bytes 245768 | tf_op jit(solution)/shard_map/ppermute | solution.py:480
  67.9 8.9 %collective-permute-start.8 = (bf16[320,128]{1,0:T(8,128)(2,1)S(1)}, bf16[320,128]{1,0:T(8,128)(2,1)S(1)}, u32[]{:S(2)}, u32[]{:S(2)}) collective-permute-start(bf16[320,128]{1,0:T(8,128)(2,1)S(1)} %get-tuple-element.55), channel_id=1, source_target_pairs={{128,64},{144,80},{160,96},{176,112},{129,65},{145,81},{161,97},{1... | collective-permute-start | bytes 245768 | tf_op jit(solution)/shard_map/ppermute | solution.py:480
  78.5 6.9 %collective-permute-start.10 = (bf16[640,128]{1,0:T(8,128)(2,1)S(1)}, bf16[640,128]{1,0:T(8,128)(2,1)S(1)}, u32[]{:S(2)}, u32[]{:S(2)}) collective-permute-start(bf16[640,128]{1,0:T(8,128)(2,1)S(1)} %get-tuple-element.59), channel_id=1, source_target_pairs={{0,16},{16,0},{32,48},{48,32},{64,80},{80,64},{96,112},{112,96},{1... | collective-permute-start | bytes 491528 | tf_op jit(solution)/shard_map/ppermute | solution.py:483
  80.9 7.4 %collective-permute-start.11 = (bf16[640,128]{1,0:T(8,128)(2,1)S(1)}, bf16[640,128]{1,0:T(8,128)(2,1)S(1)}, u32[]{:S(2)}, u32[]{:S(2)}) collective-permute-start(bf16[640,128]{1,0:T(8,128)(2,1)S(1)} %get-tuple-element.60), channel_id=1, source_target_pairs={{0,32},{16,48},{32,0},{48,16},{64,96},{80,112},{96,64},{112,80},{1... | collective-permute-start | bytes 491528 | tf_op jit(solution)/shard_map/ppermute | solution.py:483
  84.0 7.7 %collective-permute-start.12 = (bf16[640,128]{1,0:T(8,128)(2,1)S(1)}, bf16[640,128]{1,0:T(8,128)(2,1)S(1)}, u32[]{:S(2)}, u32[]{:S(2)}) collective-permute-start(bf16[640,128]{1,0:T(8,128)(2,1)S(1)} %get-tuple-element.61), channel_id=1, source_target_pairs={{0,48},{16,32},{32,16},{48,0},{64,112},{80,96},{96,80},{112,64},{1... | collective-permute-start | bytes 491528 | tf_op jit(solution)/shard_map/ppermute | solution.py:483
  93.3 13.2 %collective-permute-start.14 = (bf16[4,320,128]{2,1,0:T(8,128)(2,1)S(1)}, bf16[4,320,128]{2,1,0:T(8,128)(2,1)S(1)}, u32[]{:S(2)}, u32[]{:S(2)}) collective-permute-start(bf16[4,320,128]{2,1,0:T(8,128)(2,1)S(1)} %get-tuple-element.68.tops), channel_id=1, source_target_pairs={{0,16},{16,32},{32,48},{48,64},{64,80},{80,96},{96,112},{112,128},... | collective-permute-start | bytes 983048 | tf_op jit(solution)/shard_map/ppermute | solution.py:541
  97.8 8.7 %collective-permute-start.13 = (bf16[2,320,128]{2,1,0:T(8,128)(2,1)S(1)}, bf16[2,320,128]{2,1,0:T(8,128)(2,1)S(1)}, u32[]{:S(2)}, u32[]{:S(2)}) collective-permute-start(bf16[2,320,128]{2,1,0:T(8,128)(2,1)S(1)} %get-tuple-element.72), channel_id=1, source_target_pairs={{1,2},{2,1},{3,4},{4,3},{5,6},{6,5},{7,8},{8,7},{9,10},{10,9},{11,... | collective-permute-start | bytes 491528 | tf_op jit(solution)/shard_map/ppermute | solution.py:553
  99.7 6.8 %collective-permute-start.15 = (bf16[2,320,128]{2,1,0:T(8,128)(2,1)S(1)}, bf16[2,320,128]{2,1,0:T(8,128)(2,1)S(1)}, u32[]{:S(2)}, u32[]{:S(2)}) collective-permute-start(bf16[2,320,128]{2,1,0:T(8,128)(2,1)S(1)} %get-tuple-element.73), channel_id=1, source_target_pairs={{0,1},{1,0},{2,3},{3,2},{4,5},{5,4},{6,7},{7,6},{8,9},{9,8},{10,11... | collective-permute-start | bytes 491528 | tf_op jit(solution)/shard_map/ppermute | solution.py:554
